TPU v7x, 512 devices: a whole 4x8x8 slice. The times are simulated.
512 devices in a mesh: req: 64 (over x, y, core), kv: 8 (over z).
Axes of the slice: x: 4, y: 8, z: 8, core: 2. Of those that a mesh axis runs over, the one named last changes fastest.
Arguments:
- tokens: bfloat16 [64, 4096], P('req'), may hold values from -6 to 6
- attn_gain: float32 [4096], replicated, may hold values from 0.5 to 1.5
- mlp_gain: float32 [4096], replicated, may hold values from 0.5 to 1.5
- w_query: bfloat16 [4096, 4096], P('req', 'kv'), may hold values from -0.09375 to 0.09375
- w_key: bfloat16 [4096, 1024], P('req', 'kv'), may hold values from -0.09375 to 0.09375
- w_value: bfloat16 [4096, 1024], P('req', 'kv'), may hold values from -0.09375 to 0.09375
- w_out: bfloat16 [4096, 4096], P('kv', 'req'), may hold values from -0.09375 to 0.09375
- w_gate: bfloat16 [4096, 14336], P('kv', 'req'), may hold values from -0.09375 to 0.09375
- w_up: bfloat16 [4096, 14336], P('kv', 'req'), may hold values from -0.09375 to 0.09375
- w_down: bfloat16 [14336, 4096], P('req', 'kv'), may hold values from -0.046875 to 0.046875
- cache_keys: bfloat16 [1024, 256, 1024], P('req', None, 'kv')
- cache_values: bfloat16 [1024, 256, 1024], P('req', None, 'kv'), may hold values from -6 to 6
- slot_owner: int32 [1024], P('req'), may hold values from 0 to 63, as said below
- slot_fill: int32 [1024], P('req'), may hold values from 0 to 256, as said below
Outputs:
- out: bfloat16 [64, 4096], P('req', 'kv')
Inputs may be any that keep to these rules, and one draw needn't show every extreme that they name: `slot_owner`: every request owns one slot or more. `slot_fill`: every index of req holds one full slot and one empty slot.
All inputs are finite; a program needn't handle non-finite values.
Results may differ from a plain program's by a relative error of at most 0.013.
The roundings to bfloat16 on the way count: a program that leaves them out, or rounds other values in their place, can miss the bound.
Values may be sent and summed in bfloat16 or wider, within the bound.
A program may use at most 64 MiB of HBM per device.

v0:
```python
import jax
import jax.numpy as jnp
from jax import lax
from jax.sharding import PartitionSpec as P

HQ = 32
HK = 8
DH = 128
EPS = 1e-05
NEG = -1e30


def joined_2(array, axis, combine):
    everything = jax.tree.map(lambda part: lax.all_gather(part, axis), array)
    initial = jax.tree.map(lambda part: part[0], everything)

    def step(k, so_far):
        return combine(so_far, jax.tree.map(lambda part: part[k], everything))

    return lax.fori_loop(1, lax.axis_size(axis), step, initial)


def rms_norm(rows, gain):
    mean = jnp.mean(rows * rows, axis=-1, keepdims=True)
    return (rows * lax.rsqrt(mean + EPS) * gain).astype(jnp.bfloat16)


def combine_parts(first, second):
    highest = jnp.maximum(first[0], second[0])
    left = jnp.exp(first[0] - highest)
    right = jnp.exp(second[0] - highest)
    return (
        highest,
        first[1] * left + second[1] * right,
        first[2] * left[..., None] + second[2] * right[..., None],
    )


def finish_heads(run_max, run_total, run_acc, query, new_key, new_value, scale):
    own_score = (
        jnp.sum(query.astype(jnp.float32) * new_key.astype(jnp.float32)[:, :, None, :], axis=-1)
        * scale
    )
    highest = jnp.maximum(run_max, own_score)
    older = jnp.exp(run_max - highest)
    fresh = jnp.exp(own_score - highest)
    total = run_total * older + fresh
    accum = (
        run_acc * older[..., None] + fresh[..., None] * new_value.astype(jnp.float32)[:, :, None, :]
    )
    return (accum / total[..., None]).astype(jnp.bfloat16).reshape(query.shape[0], -1)


def per_device(
    tokens,
    attn_gain,
    mlp_gain,
    w_query,
    w_key,
    w_value,
    w_out,
    w_gate,
    w_up,
    w_down,
    cache_keys,
    cache_values,
    slot_owner,
    slot_fill,
):
    req_count = lax.axis_size("req")
    kv_count = lax.axis_size("kv")
    local_rows = tokens.shape[0]
    requests = local_rows * req_count
    group = HQ // HK
    kv_local = cache_keys.shape[2] // DH
    scale = DH ** (-0.5)
    resid_in = tokens.astype(jnp.float32)
    normed = rms_norm(resid_in, attn_gain)
    feature_cols = lax.all_to_all(normed, "req", split_axis=1, concat_axis=0, tiled=True)
    joined = jnp.concatenate([w_query, w_key, w_value], axis=1)
    width_q = w_query.shape[1]
    width_k = w_key.shape[1]
    partial_proj = jnp.dot(feature_cols, joined, preferred_element_type=jnp.float32)
    projected = lax.psum(partial_proj, "req").astype(jnp.bfloat16)
    query = projected[:, :width_q].reshape(requests, kv_local, group, DH)
    new_key = projected[:, width_q : width_q + width_k].reshape(requests, kv_local, DH)
    new_value = projected[:, width_q + width_k :].reshape(requests, kv_local, DH)
    slots = cache_keys.shape[0]
    block_len = cache_keys.shape[1]
    keys_four = cache_keys.reshape(slots, block_len, kv_local, DH)
    values_four = cache_values.reshape(slots, block_len, kv_local, DH)
    slot_query = jnp.take(query, slot_owner, axis=0)
    scores = (
        jnp.einsum("skgd,sbkd->skgb", slot_query, keys_four, preferred_element_type=jnp.float32)
        * scale
    )
    valid = (lax.broadcasted_iota(jnp.int32, (slots, block_len), 1) < slot_fill[:, None])[
        :, None, None, :
    ]
    masked = jnp.where(valid, scores, NEG)
    slot_max = jnp.max(masked, axis=-1)
    prob = jnp.where(valid, jnp.exp(masked - slot_max[..., None]), 0.0)
    slot_total = jnp.sum(prob, axis=-1)
    slot_acc = jnp.einsum(
        "skgb,sbkd->skgd",
        prob.astype(jnp.bfloat16),
        values_four,
        preferred_element_type=jnp.float32,
    )
    run_max = jnp.full((requests, kv_local, group), NEG, jnp.float32).at[slot_owner].max(slot_max)
    rescale = jnp.exp(slot_max - run_max[slot_owner])
    run_total = (
        jnp.zeros((requests, kv_local, group), jnp.float32).at[slot_owner].add(slot_total * rescale)
    )
    run_acc = (
        jnp.zeros((requests, kv_local, group, DH), jnp.float32)
        .at[slot_owner]
        .add(slot_acc * rescale[..., None])
    )
    merged_max, merged_total, merged_acc = joined_2(
        (run_max, run_total, run_acc), "req", combine_parts
    )
    heads = finish_heads(merged_max, merged_total, merged_acc, query, new_key, new_value, scale)
    out_part = jnp.dot(heads, w_out, preferred_element_type=jnp.float32)
    head_total = lax.psum(out_part, "kv")
    attn_rows = lax.all_to_all(head_total, "req", split_axis=0, concat_axis=1, tiled=True)
    resid = resid_in + attn_rows
    normed2 = rms_norm(resid, mlp_gain)
    feature_width = normed2.shape[1] // kv_count
    kv_start = lax.axis_index("kv") * feature_width
    feature_block = lax.dynamic_slice_in_dim(normed2, kv_start, feature_width, 1)
    gate_up = jnp.concatenate([w_gate, w_up], axis=1)
    both_parts = jnp.dot(
        lax.all_gather(feature_block, "req", axis=0, tiled=True),
        gate_up,
        preferred_element_type=jnp.float32,
    )
    both_sums = lax.psum_scatter(
        both_parts.astype(jnp.bfloat16), "kv", scatter_dimension=0, tiled=True
    ).astype(jnp.float32)
    hidden_width = w_gate.shape[1]
    hidden = (jax.nn.silu(both_sums[:, :hidden_width]) * both_sums[:, hidden_width:]).astype(
        jnp.bfloat16
    )
    down_parts = jnp.dot(
        lax.all_gather(hidden, "kv", axis=0, tiled=True), w_down, preferred_element_type=jnp.float32
    )
    down_home = lax.psum_scatter(down_parts, "req", scatter_dimension=0, tiled=True)
    resid_block = lax.dynamic_slice_in_dim(resid, kv_start, feature_width, 1)
    return (resid_block + down_home).astype(jnp.bfloat16)


def solution(mesh):
    placed = (
        P("req", None),
        P(),
        P(),
        P("req", "kv"),
        P("req", "kv"),
        P("req", "kv"),
        P("kv", "req"),
        P("kv", "req"),
        P("kv", "req"),
        P("req", "kv"),
        P("req", None, "kv"),
        P("req", None, "kv"),
        P("req"),
        P("req"),
    )
    return jax.shard_map(
        per_device, mesh=mesh, in_specs=placed, out_specs=P("req", "kv"), check_vma=False
    )
```

profile of v0, /device:TPU:1, one launch (start us, length us, event | category | flops | bytes accessed | tf_op | source)
XLA Modules:
  0.0 840.2 jit_solution(18141316335080766035)
XLA Ops:
  6.6 1.5 multiply_reduce_fusion.2
  10.2 11.6 %all-to-all-start = ((bf16[1,64,64]{2,0,1:T(2,128)(2,1)}), bf16[1,64,64]{2,0,1:T(2,128)(2,1)S(1)}, u32[]{:S(2)}, u32[]{:S(2)}) async-start(bf16[1,64,64]{2,0,1:T(2,128)(2,1)} %all_to_all.30), calls=%async_computation | async-start | bytes 65536 | tf_op jit(solution)/shard_map/all_to_all | solution.py:79
  23.9 7.2 all-to-all-done
  32.2 241.8 %all-reduce.5 = bf16[64,768]{1,0:T(8,128)(2,1)S(1)} all-reduce(f32[64,768]{1,0:T(8,128)S(1)} %fusion.10), channel_id=1, replica_groups=mesh['req'=64,'kv'=8] {'req'}, use_global_device_ids=true, to_apply=%region_1.0 | all-reduce | flops 49152 | bytes 294912 | tf_op jit(solution)/shard_map/psum | solution.py:84
  276.4 1.5 convolution_multiply_fusion.1
  281.0 52.1 %all-gather.4 = f32[64,64,4]{1,2,0:T(4,128)S(1)} all-gather(f32[1,64,4]{1,2,0:T(4,128)S(1)} %copy.60), channel_id=3, replica_groups=mesh['req'=64,'kv'=8] {'req'}, dimensions={0}, use_global_device_ids=true | all-gather | bytes 66560 | tf_op jit(solution)/shard_map/all_gather | solution.py:14
  333.1 50.0 %all-gather.3 = f32[64,64,4]{1,2,0:T(4,128)S(1)} all-gather(f32[1,64,4]{1,2,0:T(4,128)S(1)} %copy.59), channel_id=2, replica_groups=mesh['req'=64,'kv'=8] {'req'}, dimensions={0}, use_global_device_ids=true | all-gather | bytes 66560 | tf_op jit(solution)/shard_map/all_gather | solution.py:14
  384.0 100.0 %while.19 = (s32[]{:T(128)}, f32[64,1,4]{0,2,1:T(4,128)S(1)}, f32[64,1,4]{0,2,1:T(4,128)S(1)}, f32[64,1,4,128]{3,2,1,0:T(4,128)S(1)}, f32[64,64,1,4]{1,3,2,0:T(4...) while((s32[]{:T(128)}, f32[64,1,4]{0,2,1:T(4,128)S(1)}, ...), condition=%wide.region_8.9_spmd, body=%wide.region_7.8_spmd.sunk | while | flops 100101 | bytes 412819 | solution.py:20
  384.3 1.3 fusion.60
  385.9 1.3 fusion.60
  387.5 1.3 fusion.60
  389.1 1.3 fusion.60
  390.6 1.3 fusion.60
  392.2 1.3 fusion.60
  393.8 1.3 fusion.60
  484.7 29.5 %psum.15 = f32[64,1,64]{2,0,1:T(8,128)} all-reduce(f32[64,1,64]{2,0,1:T(8,128)S(1)} %convolution_bitcast_fusion), channel_id=1, replica_groups=mesh['req'=64,'kv'=8] {'kv'}, use_global_device_ids=true, to_apply=%region_10.11 | all-reduce | flops 4096 | bytes 32768 | tf_op jit(solution)/shard_map/psum | solution.py:125
  514.3 11.5 %all-to-all-start.1 = ((f32[64,1,64]{2,1,0:T(1,128)}), f32[64,1,64]{2,1,0:T(1,128)S(1)}, u32[]{:S(2)}, u32[]{:S(2)}) async-start(f32[64,1,64]{2,1,0:T(1,128)} %bitcast.23), calls=%async_computation.1 | async-start | bytes 65536 | tf_op jit(solution)/shard_map/all_to_all | solution.py:126
  525.9 9.3 %all-to-all-done.1 = f32[64,1,64]{2,1,0:T(1,128)S(1)} async-done(((f32[64,1,64]{2,1,0:T(1,128)}), f32[64,1,64]{2,1,0:T(1,128)S(1)}, u32[]{:S(2)}, u32[]{:S(2)}) %all-to-all-start.1) | async-done | bytes 16416 | tf_op jit(solution)/shard_map/all_to_all | solution.py:126
  538.5 48.1 %all-gather.5 = bf16[64,1,512]{2,1,0:T(2,128)(2,1)S(1)} all-gather(bf16[1,1,512]{2,1,0:T(2,128)(2,1)S(1)} %fusion.40), channel_id=1, replica_groups=mesh['req'=64,'kv'=8] {'req'}, dimensions={0}, use_global_device_ids=true | all-gather | bytes 66560 | tf_op jit(solution)/shard_map/all_gather | solution.py:134
  587.6 26.7 %reduce-scatter.2.cloned.1.call-done = bf16[8,448]{1,0:T(8,128)(2,1)} async-done(((bf16[64,448]{1,0:T(8,128)(2,1)}), bf16[8,448]{1,0:T(8,128)(2,1)}) %reduce-scatter.2.cloned.1.call-update) | async-done | bytes 7184 | tf_op jit(solution)/shard_map/reduce_scatter | solution.py:138
  615.0 18.3 %all_gather.31 = bf16[64,224]{1,0:T(8,128)(2,1)S(1)} all-gather(bf16[8,224]{1,0:T(8,128)(2,1)S(1)} %fusion.34), channel_id=1, replica_groups=mesh['req'=64,'kv'=8] {'kv'}, dimensions={0}, use_global_device_ids=true | all-gather | bytes 32256 | tf_op jit(solution)/shard_map/all_gather | solution.py:146
  634.2 1.3 dynamic-slice
  635.5 196.2 %all-reduce.4.cloned.1.call-done = f32[64,512]{1,0:T(8,128)} async-done(((f32[64,512]{1,0:T(8,128)}), f32[64,512]{1,0:T(8,128)}) %all-reduce.4.cloned.1.call-update) | async-done | bytes 131088
  831.7 1.9 fusion.41
  (435 shorter events, 105.4 us)
Async XLA Ops:
  6.5 268.1 %copy-start = (bf16[16,256,128]{2,1,0:T(8,128)(2,1)S(1)}, bf16[16,256,128]{2,1,0:T(8,128)(2,1)}, u32[]{:S(2)}) copy-start(bf16[16,256,128]{2,1,0:T(8,128)(2,1)} %param.26) | copy-start | bytes 3145732
  6.5 529.9 %copy-start.3 = (bf16[1,4096]{1,0:T(2,128)(2,1)S(1)}, bf16[1,4096]{1,0:T(2,128)(2,1)}, u32[]{:S(2)}) copy-start(bf16[1,4096]{1,0:T(2,128)(2,1)} %param.16) | copy-start | bytes 24580
  6.5 478.1 %copy-start.4 = (bf16[512,64]{0,1:T(8,128)(2,1)S(1)}, bf16[512,64]{0,1:T(8,128)(2,1)}, u32[]{:S(2)}) copy-start(bf16[512,64]{0,1:T(8,128)(2,1)} %param.22) | copy-start | bytes 196612
  6.5 580.0 %copy-start.5 = (bf16[512,224]{0,1:T(8,128)(2,1)S(1)}, bf16[512,224]{0,1:T(8,128)(2,1)}, u32[]{:S(2)}) copy-start(bf16[512,224]{0,1:T(8,128)(2,1)} %param.24) | copy-start | bytes 688132
  6.5 580.0 %copy-start.6 = (bf16[512,224]{0,1:T(8,128)(2,1)S(1)}, bf16[512,224]{0,1:T(8,128)(2,1)}, u32[]{:S(2)}) copy-start(bf16[512,224]{0,1:T(8,128)(2,1)} %param.23) | copy-start | bytes 688132
  6.5 626.8 %copy-start.2 = (bf16[224,512]{1,0:T(8,128)(2,1)S(1)}, bf16[224,512]{1,0:T(8,128)(2,1)}, u32[]{:S(2)}) copy-start(bf16[224,512]{1,0:T(8,128)(2,1)} %param.25) | copy-start | bytes 688132
  10.2 20.9 %all-to-all-start = ((bf16[1,64,64]{2,0,1:T(2,128)(2,1)}), bf16[1,64,64]{2,0,1:T(2,128)(2,1)S(1)}, u32[]{:S(2)}, u32[]{:S(2)}) async-start(bf16[1,64,64]{2,0,1:T(2,128)(2,1)} %all_to_all.30), calls=%async_computation | async-start | bytes 65536 | tf_op jit(solution)/shard_map/all_to_all | solution.py:79
  21.8 361.3 %all-gather.8.cloned.1.call-start = ((), (), s32[]{:S(2)}) async-start(), calls=%async_computation.4 | async-start | bytes 8519680 | tf_op jit(solution)/shard_map/all_gather | solution.py:14
  279.0 0.7 copy-start.1
  514.3 20.8 %all-to-all-start.1 = ((f32[64,1,64]{2,1,0:T(1,128)}), f32[64,1,64]{2,1,0:T(1,128)S(1)}, u32[]{:S(2)}, u32[]{:S(2)}) async-start(f32[64,1,64]{2,1,0:T(1,128)} %bitcast.23), calls=%async_computation.1 | async-start | bytes 65536 | tf_op jit(solution)/shard_map/all_to_all | solution.py:126
  525.8 88.5 %reduce-scatter.2.cloned.1.call-start = ((), (), s32[]{:S(2)}) async-start(), calls=%async_computation.3 | async-start | bytes 73728 | tf_op jit(solution)/shard_map/reduce_scatter | solution.py:138
  587.5 244.2 %all-reduce.4.cloned.1.call-start = ((), (), s32[]{:S(2)}) async-start(), calls=%async_computation.5 | async-start | bytes 262144
Sparse Core Ops, SparseCore 0:
  279.8 90.5 all-gather.7
  587.6 26.5 reduce-scatter.1
  634.3 197.3 all-reduce.3
where the time goes:
time: 842 us; the launch traced here: 840 us
  blocking collectives  440 us (52%)
  waiting for transfers between devices  239 us (28%)
  other arithmetic  97.7 us (12%)
  starting transfers between devices  23.2 us (3%)
  local copies, waits for them, and re-layouts  18.2 us (2%)
  between operations  14.7 us (2%)
    psum x1, blocking collectives, per_device(): projected = lax.psum(partial_proj, 'req').astype(jnp.bfloat16)  242 us
    unnamed x4, waiting for transfers between devices  196 us
    all_gather x2, blocking collectives, joined_2(): everything = jax.tree.map(lambda part: lax.all_gather(part, axis), array)  102 us
    add x63, other arithmetic, combine_parts(): first[2] * left[..., None] + second[2] * right[..., None]  83.3 us
    all_gather x1, blocking collectives, per_device(): lax.all_gather(feature_block, 'req', axis=0, tiled=True)  48.1 us
    psum x1, blocking collectives, per_device(): head_total = lax.psum(out_part, 'kv')  29.5 us
    reduce_scatter x1, waiting for transfers between devices, per_device(): lax.psum_scatter(both_parts.astype(jnp.bfloat16), 'kv', scatter_dimension...  26.7 us
    all_gather x1, blocking collectives, per_device(): lax.all_gather(hidden, 'kv', axis=0, tiled=True)  18.3 us
  transfers between devices with their start and end apart: 5, of which 4 were waited for; matrix products, arithmetic and copies ran while one was open for 1% of the time, Pallas kernels for 0%

commit v1 on v0

--- a/solution.py
+++ b/solution.py
@@ -2,6 +2,7 @@
 import jax.numpy as jnp
 from jax import lax
 from jax.sharding import PartitionSpec as P
+from jax.lax import all_to_all, axis_size
 
 HQ = 32
 HK = 8
@@ -131,7 +132,9 @@
     feature_block = lax.dynamic_slice_in_dim(normed2, kv_start, feature_width, 1)
     gate_up = jnp.concatenate([w_gate, w_up], axis=1)
     both_parts = jnp.dot(
-        lax.all_gather(feature_block, "req", axis=0, tiled=True),
+        jnp.concatenate(
+            all_to_all(jnp.stack([feature_block for _ in range(axis_size("req"))]), "req", 0, 0), 0
+        ),
         gate_up,
         preferred_element_type=jnp.float32,
     )

time: 842 us -> 808 us (0.960)
  blocking collectives: 440 us -> 405 us
    all_gather x1 -> x0, blocking collectives: 48.1 us -> none  [per_device(): lax.all_gather(feature_block, 'req', axis=0, tiled=True)]
    all_to_all x0 -> x1, blocking collectives: none -> 13.8 us  [per_device(): all_to_all(jnp.stack([feature_block for _ in range(axis_size('req'))]), '...]
where the time goes in v1:
time: 808 us; the launch traced here: 807 us
  blocking collectives  405 us (50%)
  waiting for transfers between devices  238 us (29%)
  other arithmetic  98.7 us (12%)
  starting transfers between devices  23.2 us (3%)
  local copies, waits for them, and re-layouts  18.8 us (2%)
  between operations  14.8 us (2%)
    psum x1, blocking collectives, per_device(): projected = lax.psum(partial_proj, 'req').astype(jnp.bfloat16)  242 us
    unnamed x4, waiting for transfers between devices  196 us
    all_gather x2, blocking collectives, joined_2(): everything = jax.tree.map(lambda part: lax.all_gather(part, axis), array)  102 us
    add x63, other arithmetic, combine_parts(): first[2] * left[..., None] + second[2] * right[..., None]  83.3 us
    psum x1, blocking collectives, per_device(): head_total = lax.psum(out_part, 'kv')  29.5 us
    reduce_scatter x1, waiting for transfers between devices, per_device(): lax.psum_scatter(both_parts.astype(jnp.bfloat16), 'kv', scatter_dimension...  25.5 us
    all_gather x1, blocking collectives, per_device(): lax.all_gather(hidden, 'kv', axis=0, tiled=True)  18.3 us
  transfers between devices with their start and end apart: 5, of which 4 were waited for; matrix products, arithmetic and copies ran while one was open for 1% of the time, Pallas kernels for 0%

profile of v1, /device:TPU:1, one launch (start us, length us, event | category | flops | bytes accessed | tf_op | source)
XLA Modules:
  0.0 806.6 jit_solution(7552972818271201791)
XLA Ops:
  6.6 1.5 multiply_reduce_fusion.2
  10.2 11.6 %all-to-all-start = ((bf16[1,64,64]{2,0,1:T(2,128)(2,1)}), bf16[1,64,64]{2,0,1:T(2,128)(2,1)S(1)}, u32[]{:S(2)}, u32[]{:S(2)}) async-start(bf16[1,64,64]{2,0,1:T(2,128)(2,1)} %all_to_all.34), calls=%async_computation | async-start | bytes 65536 | tf_op jit(solution)/shard_map/all_to_all | solution.py:80
  23.9 7.2 all-to-all-done
  32.2 241.8 %all-reduce.5 = bf16[64,768]{1,0:T(8,128)(2,1)S(1)} all-reduce(f32[64,768]{1,0:T(8,128)S(1)} %fusion.10), channel_id=1, replica_groups=mesh['req'=64,'kv'=8] {'req'}, use_global_device_ids=true, to_apply=%region_1.0 | all-reduce | flops 49152 | bytes 294912 | tf_op jit(solution)/shard_map/psum | solution.py:85
  276.4 1.5 convolution_multiply_fusion.1
  281.0 52.1 %all-gather.4 = f32[64,64,4]{1,2,0:T(4,128)S(1)} all-gather(f32[1,64,4]{1,2,0:T(4,128)S(1)} %copy.60), channel_id=3, replica_groups=mesh['req'=64,'kv'=8] {'req'}, dimensions={0}, use_global_device_ids=true | all-gather | bytes 66560 | tf_op jit(solution)/shard_map/all_gather | solution.py:15
  333.1 50.0 %all-gather.3 = f32[64,64,4]{1,2,0:T(4,128)S(1)} all-gather(f32[1,64,4]{1,2,0:T(4,128)S(1)} %copy.59), channel_id=2, replica_groups=mesh['req'=64,'kv'=8] {'req'}, dimensions={0}, use_global_device_ids=true | all-gather | bytes 66560 | tf_op jit(solution)/shard_map/all_gather | solution.py:15
  384.0 100.0 %while.19 = (s32[]{:T(128)}, f32[64,1,4]{0,2,1:T(4,128)S(1)}, f32[64,1,4]{0,2,1:T(4,128)S(1)}, f32[64,1,4,128]{3,2,1,0:T(4,128)S(1)}, f32[64,64,1,4]{1,3,2,0:T(4...) while((s32[]{:T(128)}, f32[64,1,4]{0,2,1:T(4,128)S(1)}, ...), condition=%wide.region_8.9_spmd, body=%wide.region_7.8_spmd.sunk | while | flops 100101 | bytes 412819 | solution.py:21
  384.3 1.3 fusion.60
  385.9 1.3 fusion.60
  387.5 1.3 fusion.60
  389.1 1.3 fusion.60
  390.6 1.3 fusion.60
  392.2 1.3 fusion.60
  393.8 1.3 fusion.60
  484.7 29.5 %psum.15 = f32[64,1,64]{2,0,1:T(8,128)} all-reduce(f32[64,1,64]{2,0,1:T(8,128)S(1)} %convolution_bitcast_fusion), channel_id=1, replica_groups=mesh['req'=64,'kv'=8] {'kv'}, use_global_device_ids=true, to_apply=%region_10.11 | all-reduce | flops 4096 | bytes 32768 | tf_op jit(solution)/shard_map/psum | solution.py:126
  514.3 11.5 %all-to-all-start.1 = ((f32[64,1,64]{2,1,0:T(1,128)}), f32[64,1,64]{2,1,0:T(1,128)S(1)}, u32[]{:S(2)}, u32[]{:S(2)}) async-start(f32[64,1,64]{2,1,0:T(1,128)} %bitcast.23), calls=%async_computation.1 | async-start | bytes 65536 | tf_op jit(solution)/shard_map/all_to_all | solution.py:127
  525.9 9.3 %all-to-all-done.1 = f32[64,1,64]{2,1,0:T(1,128)S(1)} async-done(((f32[64,1,64]{2,1,0:T(1,128)}), f32[64,1,64]{2,1,0:T(1,128)S(1)}, u32[]{:S(2)}, u32[]{:S(2)}) %all-to-all-start.1) | async-done | bytes 16416 | tf_op jit(solution)/shard_map/all_to_all | solution.py:127
  540.1 13.8 %all_to_all.38 = bf16[64,2,256]{2,1,0:T(2,128)(2,1)S(1)} all-to-all(bf16[64,2,256]{2,1,0:T(2,128)(2,1)S(1)} %reshape.317), channel_id=1, replica_groups=mesh['req'=64,'kv'=8] {'req'}, dimensions={0} | all-to-all | bytes 131072 | tf_op jit(solution)/shard_map/all_to_all | solution.py:136
  554.9 25.5 %reduce-scatter.2.cloned.1.call-done = bf16[8,448]{1,0:T(8,128)(2,1)} async-done(((bf16[64,448]{1,0:T(8,128)(2,1)}), bf16[8,448]{1,0:T(8,128)(2,1)}) %reduce-scatter.2.cloned.1.call-update) | async-done | bytes 7184 | tf_op jit(solution)/shard_map/reduce_scatter | solution.py:141
  581.2 18.3 %all_gather.27 = bf16[64,224]{1,0:T(8,128)(2,1)S(1)} all-gather(bf16[8,224]{1,0:T(8,128)(2,1)S(1)} %fusion.34), channel_id=1, replica_groups=mesh['req'=64,'kv'=8] {'kv'}, dimensions={0}, use_global_device_ids=true | all-gather | bytes 32256 | tf_op jit(solution)/shard_map/all_gather | solution.py:149
  600.4 1.3 dynamic-slice
  601.7 196.4 %all-reduce.4.cloned.1.call-done = f32[64,512]{1,0:T(8,128)} async-done(((f32[64,512]{1,0:T(8,128)}), f32[64,512]{1,0:T(8,128)}) %all-reduce.4.cloned.1.call-update) | async-done | bytes 131088
  798.1 1.9 fusion.40
  (440 shorter events, 107.1 us)
Async XLA Ops:
  6.5 268.1 %copy-start = (bf16[16,256,128]{2,1,0:T(8,128)(2,1)S(1)}, bf16[16,256,128]{2,1,0:T(8,128)(2,1)}, u32[]{:S(2)}) copy-start(bf16[16,256,128]{2,1,0:T(8,128)(2,1)} %param.26) | copy-start | bytes 3145732
  6.5 529.9 %copy-start.3 = (bf16[1,4096]{1,0:T(2,128)(2,1)S(1)}, bf16[1,4096]{1,0:T(2,128)(2,1)}, u32[]{:S(2)}) copy-start(bf16[1,4096]{1,0:T(2,128)(2,1)} %param.16) | copy-start | bytes 24580
  6.5 478.1 %copy-start.4 = (bf16[512,64]{0,1:T(8,128)(2,1)S(1)}, bf16[512,64]{0,1:T(8,128)(2,1)}, u32[]{:S(2)}) copy-start(bf16[512,64]{0,1:T(8,128)(2,1)} %param.22) | copy-start | bytes 196612
  6.5 547.4 %copy-start.5 = (bf16[512,224]{0,1:T(8,128)(2,1)S(1)}, bf16[512,224]{0,1:T(8,128)(2,1)}, u32[]{:S(2)}) copy-start(bf16[512,224]{0,1:T(8,128)(2,1)} %param.24) | copy-start | bytes 688132
  6.5 547.4 %copy-start.6 = (bf16[512,224]{0,1:T(8,128)(2,1)S(1)}, bf16[512,224]{0,1:T(8,128)(2,1)}, u32[]{:S(2)}) copy-start(bf16[512,224]{0,1:T(8,128)(2,1)} %param.23) | copy-start | bytes 688132
  6.5 593.0 %copy-start.2 = (bf16[224,512]{1,0:T(8,128)(2,1)S(1)}, bf16[224,512]{1,0:T(8,128)(2,1)}, u32[]{:S(2)}) copy-start(bf16[224,512]{1,0:T(8,128)(2,1)} %param.25) | copy-start | bytes 688132
  10.2 20.9 %all-to-all-start = ((bf16[1,64,64]{2,0,1:T(2,128)(2,1)}), bf16[1,64,64]{2,0,1:T(2,128)(2,1)S(1)}, u32[]{:S(2)}, u32[]{:S(2)}) async-start(bf16[1,64,64]{2,0,1:T(2,128)(2,1)} %all_to_all.34), calls=%async_computation | async-start | bytes 65536 | tf_op jit(solution)/shard_map/all_to_all | solution.py:80
  21.8 361.3 %all-gather.7.cloned.1.call-start = ((), (), s32[]{:S(2)}) async-start(), calls=%async_computation.5 | async-start | bytes 8519680 | tf_op jit(solution)/shard_map/all_gather | solution.py:15
  279.0 0.7 copy-start.1
  514.3 20.8 %all-to-all-start.1 = ((f32[64,1,64]{2,1,0:T(1,128)}), f32[64,1,64]{2,1,0:T(1,128)S(1)}, u32[]{:S(2)}, u32[]{:S(2)}) async-start(f32[64,1,64]{2,1,0:T(1,128)} %bitcast.23), calls=%async_computation.1 | async-start | bytes 65536 | tf_op jit(solution)/shard_map/all_to_all | solution.py:127
  525.8 54.7 %reduce-scatter.2.cloned.1.call-start = ((), (), s32[]{:S(2)}) async-start(), calls=%async_computation.4 | async-start | bytes 73728 | tf_op jit(solution)/shard_map/reduce_scatter | solution.py:141
  554.9 243.2 %all-reduce.4.cloned.1.call-start = ((), (), s32[]{:S(2)}) async-start(), calls=%async_computation.6 | async-start | bytes 262144
Sparse Core Ops, SparseCore 0:
  279.8 90.5 all-gather.6
  555.0 25.4 reduce-scatter.1
  600.5 197.5 all-reduce.3
